TPU v7x, 32 devices: a whole 2x2x4 slice. The times are simulated.
32 devices in a mesh: groups: 2 (over y), role: 4 (over x, core), tp: 4 (over z).
Axes of the slice: x: 2, y: 2, z: 4, core: 2. Of those that a mesh axis runs over, the one named last changes fastest.
Arguments:
- residual: bfloat16 [64, 8192], P(('groups', 'tp'), 'role'), parts along dimension 0, may hold values from -20 to 20
- attn_gain: float32 [8192], P('role'), may hold values from 0.1 to 1.9
- w_query: bfloat16 [8192, 4096], P('role', 'tp'), may hold values from -0.0625 to 0.0625
- w_key: bfloat16 [8192, 512], P('role', 'tp'), may hold values from -0.0625 to 0.0625
- w_value: bfloat16 [8192, 512], P('role', 'tp'), may hold values from -0.0625 to 0.0625
- w_output: bfloat16 [4096, 8192], P('tp', 'role'), may hold values from -0.09375 to 0.09375
- cache_keys: bfloat16 [64, 256, 512], P(('groups', 'role', 'tp')), parts along dimension 0, may hold values from -300 to 300
- cache_values: bfloat16 [64, 256, 512], P(('groups', 'role', 'tp')), parts along dimension 0, may hold values from -12 to 12
- lengths: int32 [64], P(('groups', 'role', 'tp')), parts along dimension 0, may hold values from 2 to 256
- served: int32 [64], P('groups'), parts along dimension 0, may hold values 0 or 1
- ffn_gain: float32 [8192], P('role'), may hold values from 0.1 to 1.9
- w_gate: bfloat16 [8192, 14336], P('role', 'tp'), may hold values from -0.0625 to 0.0625
- w_up: bfloat16 [8192, 14336], P('role', 'tp'), may hold values from -0.0625 to 0.0625
- w_down: bfloat16 [14336, 8192], P('tp', 'role'), may hold values from -0.046875 to 0.046875
Outputs:
- layer_out: bfloat16 [64, 8192], P(('groups', 'tp'), 'role'), parts along dimension 0
There are 2 independent parts, one for each index of `groups`. A program takes and returns all parts, laid end to end along the dimension named above; an argument that names none is the same for every part. Nothing has to cross between parts.
Inputs may be any that keep to these rules, and one draw needn't show every extreme that they name: Each request's new token stands at position lengths; cached positions from lengths on are unused.
All inputs are finite; a program needn't handle non-finite values.
Results may differ from a plain program's by a relative error of at most 0.024.
Values may be sent and summed in bfloat16 or wider, within the bound.
No kernel may reach another device: no remote copies, remote signals or barrier semaphores. Data moves between devices by JAX's collectives and lax.ppermute only.
A program may use at most 128 MiB of HBM per device.

v0:
```python
import jax
import jax.numpy as jnp
from jax import lax
from jax.sharding import PartitionSpec as P

D = 8192
HEADS = 32
KV_HEADS = 4
HEAD_DIM = 128
WINDOW = 256
GROUP = 8
epsilon = 1e-05
rope_base = 500000.0


def rotate(vectors, positions):
    halfway = vectors.shape[-1] // 2
    frequency = jnp.power(
        jnp.float32(rope_base), -jnp.arange(halfway, dtype=jnp.float32) * 2.0 / vectors.shape[-1]
    )
    angles = positions.astype(jnp.float32)[:, None, None] * frequency[None, None, :]
    cosine = jnp.cos(angles)
    sine_part = jnp.sin(angles)
    leading = vectors[..., :halfway]
    trailing = vectors[..., halfway:]
    return jnp.concatenate(
        [leading * cosine - trailing * sine_part, trailing * cosine + leading * sine_part], axis=-1
    )


def attend(queries, new_key, new_value, keys, values, lengths):
    batch_rows = queries.shape[0]
    factor = HEAD_DIM ** (-0.5)
    grouped = queries.reshape(batch_rows, KV_HEADS, GROUP, HEAD_DIM)
    key_blocks = keys.reshape(batch_rows, WINDOW, KV_HEADS, HEAD_DIM)
    value_blocks = values.reshape(batch_rows, WINDOW, KV_HEADS, HEAD_DIM)
    scores = (
        jnp.einsum("nkgd,nwkd->nkgw", grouped, key_blocks, preferred_element_type=jnp.float32)
        * factor
    )
    self_score = (
        jnp.einsum("nkgd,nkd->nkg", grouped, new_key, preferred_element_type=jnp.float32) * factor
    )
    usable = jnp.arange(WINDOW, dtype=jnp.int32)[None, :] < lengths[:, None]
    scores = jnp.where(usable[:, None, None, :], scores, -jnp.inf)
    highest = jnp.maximum(jnp.max(scores, axis=-1), self_score)
    weights = jnp.exp(scores - highest[..., None])
    self_weight = jnp.exp(self_score - highest)
    denominator = jnp.sum(weights, axis=-1) + self_weight
    chances = (weights / denominator[..., None]).astype(jnp.bfloat16)
    self_chance = (self_weight / denominator).astype(jnp.bfloat16)
    attended = jnp.einsum(
        "nkgw,nwkd->nkgd", chances, value_blocks, preferred_element_type=jnp.float32
    )
    attended = (
        attended
        + self_chance.astype(jnp.float32)[..., None] * new_value.astype(jnp.float32)[:, :, None, :]
    )
    return attended.reshape(batch_rows, HEADS * HEAD_DIM).astype(jnp.bfloat16)


def feed_forward(middle, ffn_gain, w_gate, w_up, w_down):
    widened = middle.astype(jnp.float32)
    squares = lax.psum(jnp.sum(widened * widened, axis=1), "role")
    inverse = lax.rsqrt(squares / D + epsilon)
    mid_normed = (widened * inverse[:, None] * ffn_gain[None, :]).astype(jnp.bfloat16)
    gate_part = jnp.dot(mid_normed, w_gate, preferred_element_type=jnp.float32)
    up_part = jnp.dot(mid_normed, w_up, preferred_element_type=jnp.float32)
    gate_total, up_total = (
        lax.psum(gate_part.astype(jnp.bfloat16), "role").astype(jnp.float32),
        lax.psum(up_part.astype(jnp.bfloat16), "role").astype(jnp.float32),
    )
    hidden = (jax.nn.silu(gate_total) * up_total).astype(jnp.bfloat16)
    down_terms = jnp.dot(hidden, w_down, preferred_element_type=jnp.float32)
    return lax.psum_scatter(
        down_terms.astype(jnp.bfloat16), "tp", scatter_dimension=0, tiled=True
    ).astype(jnp.float32)


def local(
    residual,
    attn_gain,
    w_query,
    w_key,
    w_value,
    w_output,
    cache_keys,
    cache_values,
    lengths,
    served,
    ffn_gain,
    w_gate,
    w_up,
    w_down,
):
    own_rows = residual.shape[0]
    tp_count = lax.axis_size("tp")
    row_start = lax.axis_index("tp") * own_rows
    live_own = lax.dynamic_slice_in_dim(served, row_start, own_rows, 0).astype(jnp.float32)[:, None]
    rows_all = lax.all_gather(residual, "tp", axis=0, tiled=True)
    widened = rows_all.astype(jnp.float32)
    squares = lax.psum(jnp.sum(widened * widened, axis=1), "role")
    inverse = lax.rsqrt(squares / D + epsilon)
    normed = (widened * inverse[:, None] * attn_gain[None, :]).astype(jnp.bfloat16)
    partial_value = jnp.concatenate(
        [
            jnp.dot(normed, w_query, preferred_element_type=jnp.float32),
            jnp.dot(normed, w_key, preferred_element_type=jnp.float32),
            jnp.dot(normed, w_value, preferred_element_type=jnp.float32),
        ],
        axis=1,
    )
    summed = lax.psum_scatter(
        partial_value.astype(jnp.bfloat16), "role", scatter_dimension=0, tiled=True
    ).astype(jnp.float32)
    gathered = lax.all_to_all(
        summed.astype(jnp.bfloat16), "tp", split_axis=0, concat_axis=1, tiled=True
    ).astype(summed.dtype)
    local_rows = gathered.shape[0]
    query_cols = w_query.shape[1]
    kv_cols = w_key.shape[1]
    blocks = gathered.reshape(local_rows, tp_count, query_cols + 2 * kv_cols)
    queries = blocks[:, :, :query_cols].reshape(local_rows, HEADS, HEAD_DIM)
    new_key = blocks[:, :, query_cols : query_cols + kv_cols].reshape(
        local_rows, KV_HEADS, HEAD_DIM
    )
    new_value = (
        blocks[:, :, query_cols + kv_cols :]
        .reshape(local_rows, KV_HEADS, HEAD_DIM)
        .astype(jnp.bfloat16)
    )
    queries = rotate(queries, lengths).astype(jnp.bfloat16)
    new_key = rotate(new_key, lengths).astype(jnp.bfloat16)
    attended = attend(queries, new_key, new_value, cache_keys, cache_values, lengths)
    head_block = lax.all_to_all(attended, "tp", split_axis=1, concat_axis=0, tiled=True)
    attn_terms = jnp.dot(
        lax.all_gather(head_block, "role", axis=0, tiled=True),
        w_output,
        preferred_element_type=jnp.float32,
    )
    attn = lax.psum_scatter(
        attn_terms.astype(jnp.bfloat16), "tp", scatter_dimension=0, tiled=True
    ).astype(jnp.float32)
    middle_own = (residual.astype(jnp.float32) + live_own * attn).astype(jnp.bfloat16)
    middle = lax.all_gather(middle_own, "tp", axis=0, tiled=True)
    ffn = feed_forward(middle, ffn_gain, w_gate, w_up, w_down)
    return (middle_own.astype(jnp.float32) + live_own * ffn).astype(jnp.bfloat16)


def solution(mesh):
    return jax.shard_map(
        local,
        mesh=mesh,
        in_specs=(
            P(("groups", "tp"), "role"),
            P("role"),
            P("role", "tp"),
            P("role", "tp"),
            P("role", "tp"),
            P("tp", "role"),
            P(("groups", "role", "tp"), None, None),
            P(("groups", "role", "tp"), None, None),
            P(("groups", "role", "tp")),
            P("groups"),
            P("role"),
            P("role", "tp"),
            P("role", "tp"),
            P("tp", "role"),
        ),
        out_specs=P(("groups", "tp"), "role"),
        check_vma=False,
    )
```

profile of v0, /device:TPU:0, one launch (start us, length us, event | category | flops | bytes accessed | tf_op | source)
XLA Modules:
  0.0 208.5 jit_solution(7875377142544412740)
XLA Ops:
  6.5 15.4 %all_gather.9 = bf16[32,2048]{1,0:T(8,128)(2,1)S(1)} all-gather(bf16[8,2048]{1,0:T(8,128)(2,1)} %param.14), channel_id=1, replica_groups=mesh['groups'=2,'role'=4,'tp'=4] {'tp'}, dimensions={0}, use_global_device_ids=true | all-gather | bytes 163840 | tf_op jit(solution)/shard_map/all_gather | solution.py:100
  22.0 0.1 fusion.11
  22.1 5.7 %psum.28 = f32[32]{0:T(128)S(1)} all-reduce(f32[32]{0:T(128)S(1)} %fusion.11), channel_id=1, replica_groups=mesh['groups'=2,'role'=4,'tp'=4] {'role'}, use_global_device_ids=true, to_apply=%region_1.0 | all-reduce | flops 32 | bytes 256 | tf_op jit(solution)/shard_map/psum | solution.py:102
  27.8 1.3 convolution_convert_fusion.6
  29.1 1.3 convolution_convert_fusion.5
  30.4 3.1 %convolution_convert_fusion.4 = bf16[32,1024]{1,0:T(8,128)(2,1)S(1)} fusion(bf16[2048,1024]{1,0:T(8,128)(2,1)} %param.16, bf16[32,2048]{1,0:T(8,128)(2,1)S(1)} %all_gather.9, f32[2048]{0:T(1024)} %param.15, f32[32]{0:T(128)S(1)} %add_rsqrt_fusion.1), kind=kOutput, calls=%fused_computation.4 | convolution fusion | flops 134512640 | bytes 4399232 | tf_op jit(solution)/shard_map/dot_general | solution.py:107
  33.5 0.6 pad_maximum_fusion
  34.2 0.7 convert_element_type.97
  35.0 20.6 %reduce-scatter.4.cloned.1.call-done = bf16[8,1280]{1,0:T(8,128)(2,1)} async-done(((bf16[32,1280]{1,0:T(8,128)(2,1)}), bf16[8,1280]{1,0:T(8,128)(2,1)}) %reduce-scatter.4.cloned.1.call-update) | async-done | bytes 20496 | tf_op jit(solution)/shard_map/reduce_scatter | solution.py:113
  55.5 1.3 all_to_all.22
  56.9 4.6 %all-to-all-start = ((bf16[4,2,1280]{2,1,0:T(2,128)(2,1)}), bf16[4,2,1280]{2,1,0:T(2,128)(2,1)S(1)}, u32[]{:S(2)}, u32[]{:S(2)}) async-start(bf16[4,2,1280]{2,1,0:T(2,128)(2,1)} %all_to_all.22), calls=%async_computation.1 | async-start | bytes 40960 | tf_op jit(solution)/shard_map/all_to_all | solution.py:116
  61.5 0.7 iota_compare_fusion
  62.2 4.9 %all-to-all-done = bf16[4,2,1280]{2,1,0:T(2,128)(2,1)S(1)} async-done(((bf16[4,2,1280]{2,1,0:T(2,128)(2,1)}), bf16[4,2,1280]{2,1,0:T(2,128)(2,1)S(1)}, u32[]{:S(2)}, u32[]{:S(2)}) %all-to-all-start) | async-done | bytes 20512 | tf_op jit(solution)/shard_map/all_to_all | solution.py:116
  67.4 0.2 fusion.26
  67.6 0.3 fusion.37
  67.9 0.2 fusion.19
  68.2 1.3 fusion.1
  69.5 8.0 %all_to_all.29 = bf16[2,4,1024]{2,0,1:T(2,128)(2,1)S(1)} all-to-all(bf16[2,4,1024]{2,0,1:T(2,128)(2,1)S(1)} %copy.30), channel_id=1, replica_groups=mesh['groups'=2,'role'=4,'tp'=4] {'tp'}, dimensions={1} | all-to-all | bytes 32768 | tf_op jit(solution)/shard_map/all_to_all | solution.py:135
  77.5 5.2 %all_gather.10 = bf16[32,1024]{1,0:T(8,128)(2,1)S(1)} all-gather(bf16[8,1024]{1,0:T(8,128)(2,1)S(1)} %all_to_all.26), channel_id=1, replica_groups=mesh['groups'=2,'role'=4,'tp'=4] {'role'}, dimensions={0}, use_global_device_ids=true | all-gather | bytes 81920 | tf_op jit(solution)/shard_map/all_gather | solution.py:137
  82.7 3.7 %convolution_convert_fusion.3 = bf16[32,2048]{1,0:T(8,128)(2,1)} fusion(bf16[32,1024]{1,0:T(8,128)(2,1)S(1)} %all_gather.10, bf16[1024,2048]{1,0:T(8,128)(2,1)} %param.19), kind=kOutput, calls=%fused_computation.3 | convolution fusion | flops 134283264 | bytes 4390912 | tf_op jit(solution)/shard_map/dot_general | solution.py:136
  86.4 0.7 dynamic-slice_convert_fusion
  87.2 16.1 %reduce-scatter.6.cloned.1.call-done = bf16[8,2048]{1,0:T(8,128)(2,1)} async-done(((bf16[32,2048]{1,0:T(8,128)(2,1)}), bf16[8,2048]{1,0:T(8,128)(2,1)}) %reduce-scatter.6.cloned.1.call-update) | async-done | bytes 32784 | tf_op jit(solution)/shard_map/reduce_scatter | solution.py:141
  103.3 0.8 add_convert_fusion.1
  104.2 13.4 %all_gather.11 = bf16[32,2048]{1,0:T(8,128)(2,1)S(1)} all-gather(bf16[8,2048]{1,0:T(8,128)(2,1)S(1)} %add_convert_fusion.1), channel_id=1, replica_groups=mesh['groups'=2,'role'=4,'tp'=4] {'tp'}, dimensions={0}, use_global_device_ids=true | all-gather | bytes 163840 | tf_op jit(solution)/shard_map/all_gather | solution.py:145
  117.5 0.1 fusion.14
  117.7 5.7 %psum.29 = f32[32]{0:T(128)S(1)} all-reduce(f32[32]{0:T(128)S(1)} %fusion.14), channel_id=1, replica_groups=mesh['groups'=2,'role'=4,'tp'=4] {'role'}, use_global_device_ids=true, to_apply=%region_7.8 | all-reduce | flops 32 | bytes 256 | tf_op jit(solution)/shard_map/psum | solution.py:64
  123.3 8.5 %convolution_convert_fusion = bf16[32,3584]{1,0:T(8,128)(2,1)} fusion(bf16[2048,3584]{1,0:T(8,128)(2,1)} %param.26, bf16[32,2048]{1,0:T(8,128)(2,1)S(1)} %all_gather.11, f32[2048]{0:T(1024)} %param.24, f32[32]{0:T(128)S(1)} %add_rsqrt_fusion), kind=kOutput, calls=%fused_computation | convolution fusion | flops 470138880 | bytes 15048832 | tf_op jit(solution)/shard_map/dot_general | solution.py:68
  131.9 8.5 %convolution_convert_fusion.1 = bf16[32,3584]{1,0:T(8,128)(2,1)} fusion(bf16[2048,3584]{1,0:T(8,128)(2,1)} %param.25, bf16[32,2048]{1,0:T(8,128)(2,1)S(1)} %all_gather.11, f32[2048]{0:T(1024)S(1)} %copy-done.1, f32[32]{0:T(128)S(1)} %add_rsqrt_fusion), kind=kOutput, calls=%fused_computation.1 | convolution fusion | flops 470138880 | bytes 15048832 | tf_op jit(solution)/shard_map/dot_general | solution.py:67
  140.5 31.7 %all-reduce.3.cloned.1.call-done = (bf16[32,3584]{1,0:T(8,128)(2,1)}, bf16[32,3584]{1,0:T(8,128)(2,1)}) async-done(((bf16[32,3584]{1,0:T(8,128)(2,1)}, bf16[32,3584]{1,0:T(8,128)(2,1)}), (bf16[32,3584]{1,0:T(8,128)(2,1)}, bf16[32,3584]{1,0:T(8,128)(2,1)})) %all-reduce.3.cloned.1.call-update) | async-done | bytes 458768 | tf_op jit(solution)/shard_map/psum | solution.py:71
  172.2 8.7 %convolution_convert_fusion.2 = bf16[32,2048]{1,0:T(8,128)(2,1)} fusion(bf16[3584,2048]{1,0:T(8,128)(2,1)} %param.27, bf16[32,3584]{1,0:T(8,128)(2,1)} %get-tuple-element.5, bf16[32,3584]{1,0:T(8,128)(2,1)} %get-tuple-element.6), kind=kOutput, calls=%fused_computation.2 | convolution fusion | flops 470745088 | bytes 15269888 | tf_op jit(solution)/shard_map/dot_general | solution.py:74
  180.9 19.6 %reduce-scatter.8.cloned.1.call-done = bf16[8,2048]{1,0:T(8,128)(2,1)} async-done(((bf16[32,2048]{1,0:T(8,128)(2,1)}), bf16[8,2048]{1,0:T(8,128)(2,1)}) %reduce-scatter.8.cloned.1.call-update) | async-done | bytes 32784 | tf_op jit(solution)/shard_map/reduce_scatter | solution.py:75
  200.5 1.4 add_convert_fusion
  (28 shorter events, 0.6 us)
Async XLA Ops:
  6.5 61.1 %copy-start = (bf16[2,256,512]{2,1,0:T(8,128)(2,1)S(1)}, bf16[2,256,512]{2,1,0:T(8,128)(2,1)}, u32[]{:S(2)}) copy-start(bf16[2,256,512]{2,1,0:T(8,128)(2,1)} %param.20) | copy-start | bytes 1572868
  6.5 49.0 %reduce-scatter.4.cloned.1.call-start = ((), (), s32[]{:S(2)}) async-start(), calls=%async_computation.5 | async-start | bytes 102400 | tf_op jit(solution)/shard_map/reduce_scatter | solution.py:113
  56.9 10.2 %all-to-all-start = ((bf16[4,2,1280]{2,1,0:T(2,128)(2,1)}), bf16[4,2,1280]{2,1,0:T(2,128)(2,1)S(1)}, u32[]{:S(2)}, u32[]{:S(2)}) async-start(bf16[4,2,1280]{2,1,0:T(2,128)(2,1)} %all_to_all.22), calls=%async_computation.1 | async-start | bytes 40960 | tf_op jit(solution)/shard_map/all_to_all | solution.py:116
  61.5 41.9 %reduce-scatter.6.cloned.1.call-start = ((), (), s32[]{:S(2)}) async-start(), calls=%async_computation.6 | async-start | bytes 163840 | tf_op jit(solution)/shard_map/reduce_scatter | solution.py:141
  67.2 64.6 %copy-start.1 = (f32[2048]{0:T(1024)S(1)}, f32[2048]{0:T(1024)}, u32[]{:S(2)}) copy-start(f32[2048]{0:T(1024)} %param.24) | copy-start | bytes 24580
  86.4 85.8 %all-reduce.3.cloned.1.call-start = ((), (), s32[]{:S(2)}) async-start(), calls=%async_computation.8 | async-start | bytes 917504 | tf_op jit(solution)/shard_map/psum | solution.py:71
  140.4 60.1 %reduce-scatter.8.cloned.1.call-start = ((), (), s32[]{:S(2)}) async-start(), calls=%async_computation.7 | async-start | bytes 163840 | tf_op jit(solution)/shard_map/reduce_scatter | solution.py:75
Sparse Core Ops, SparseCore 0:
  34.3 21.1 reduce-scatter.3
  86.5 16.7 reduce-scatter.5
  140.5 31.5 all-reduce.2
  181.0 19.4 reduce-scatter.7
where the time goes:
time: 209 us
  waiting for transfers between devices  93 us (44%)
  blocking collectives  53.3 us (26%)
  matrix products  37 us (18%)
  between operations  13.2 us (6%)
  other arithmetic  5.94 us (3%)
  starting transfers between devices  4.69 us (2%)
    psum x1, waiting for transfers between devices, feed_forward(): lax.psum(up_part.astype(jnp.bfloat16), 'role').astype(jnp.float32)  31.7 us
    reduce_scatter x1, waiting for transfers between devices, local(): lax.psum_scatter(partial_value.astype(jnp.bfloat16), 'role', scatter_dime...  20.6 us
    reduce_scatter x1, waiting for transfers between devices, feed_forward(): lax.psum_scatter(down_terms.astype(jnp.bfloat16), 'tp', scatter_dimension...  19.6 us
    reduce_scatter x1, waiting for transfers between devices, local(): lax.psum_scatter(attn_terms.astype(jnp.bfloat16), 'tp', scatter_dimension...  16.1 us
    all_gather x1, blocking collectives, local(): rows_all = lax.all_gather(residual, 'tp', axis=0, tiled=True)  15.4 us
    all_gather x1, blocking collectives, local(): middle = lax.all_gather(middle_own, 'tp', axis=0, tiled=True)  13.4 us
    dot_general x1, matrix products, feed_forward(): down_terms = jnp.dot(hidden, w_down, preferred_element_type=jnp.float32)  8.7 us
    dot_general x1, matrix products, feed_forward(): gate_part = jnp.dot(mid_normed, w_gate, preferred_element_type=jnp.float32)  8.54 us
  transfers between devices with their start and end apart: 5, of which 5 were waited for; matrix products, arithmetic and copies ran while one was open for 1% of the time, Pallas kernels for 0%

commit v1 on v0

--- a/solution.py
+++ b/solution.py
@@ -142,7 +142,12 @@
         attn_terms.astype(jnp.bfloat16), "tp", scatter_dimension=0, tiled=True
     ).astype(jnp.float32)
     middle_own = (residual.astype(jnp.float32) + live_own * attn).astype(jnp.bfloat16)
-    middle = lax.all_gather(middle_own, "tp", axis=0, tiled=True)
+    ring = [middle_own]
+    for hop in range(3):
+        ring.append(lax.ppermute(ring[-1], "tp", [(dev, (dev + 1) % 4) for dev in range(4)]))
+    middle = jnp.roll(
+        jnp.concatenate(ring[::-1], axis=0), (lax.axis_index("tp") + 1) * ring[0].shape[0], axis=0
+    )
     ffn = feed_forward(middle, ffn_gain, w_gate, w_up, w_down)
     return (middle_own.astype(jnp.float32) + live_own * ffn).astype(jnp.bfloat16)
 

time: 209 us -> 213 us (1.019)
  waiting for transfers between devices: 93 us -> 110 us
  blocking collectives: 53.3 us -> 39.9 us
    ppermute x0 -> x3, waiting for transfers between devices: none -> 17.4 us  [local(): lax.ppermute(ring[-1], 'tp', [(dev, (dev + 1) % 4) for dev in range(4)])]
    all_gather x1 -> x0, blocking collectives: 13.4 us -> none  [local(): middle = lax.all_gather(middle_own, 'tp', axis=0, tiled=True)]
  transfers between devices with their start and end apart: 5 -> 8, of which waited for: 5 -> 8; matrix products, arithmetic and copies ran while one was open for 1% -> 1% of each run, Pallas kernels for 0% -> 0%
where the time goes in v1:
time: 213 us
  waiting for transfers between devices  110 us (52%)
  blocking collectives  39.9 us (19%)
  matrix products  37 us (17%)
  between operations  13.3 us (6%)
  other arithmetic  5.95 us (3%)
  starting transfers between devices  4.75 us (2%)
    psum x1, waiting for transfers between devices, feed_forward(): lax.psum(up_part.astype(jnp.bfloat16), 'role').astype(jnp.float32)  31.7 us
    reduce_scatter x1, waiting for transfers between devices, local(): lax.psum_scatter(partial_value.astype(jnp.bfloat16), 'role', scatter_dime...  20.6 us
    reduce_scatter x1, waiting for transfers between devices, feed_forward(): lax.psum_scatter(down_terms.astype(jnp.bfloat16), 'tp', scatter_dimension...  19.6 us
    ppermute x3, waiting for transfers between devices, local(): lax.ppermute(ring[-1], 'tp', [(dev, (dev + 1) % 4) for dev in range(4)])  17.4 us
    reduce_scatter x1, waiting for transfers between devices, local(): lax.psum_scatter(attn_terms.astype(jnp.bfloat16), 'tp', scatter_dimension...  16.2 us
    all_gather x1, blocking collectives, local(): rows_all = lax.all_gather(residual, 'tp', axis=0, tiled=True)  15.4 us
    dot_general x1, matrix products, feed_forward(): down_terms = jnp.dot(hidden, w_down, preferred_element_type=jnp.float32)  8.71 us
    dot_general x1, matrix products, feed_forward(): gate_part = jnp.dot(mid_normed, w_gate, preferred_element_type=jnp.float32)  8.54 us
  transfers between devices with their start and end apart: 8, of which 8 were waited for; matrix products, arithmetic and copies ran while one was open for 1% of the time, Pallas kernels for 0%

profile of v1, /device:TPU:0, one launch (start us, length us, event | category | flops | bytes accessed | tf_op | source)
XLA Modules:
  0.0 212.7 jit_solution(6557733546753841739)
XLA Ops:
  6.5 15.4 %all_gather.6 = bf16[32,2048]{1,0:T(8,128)(2,1)S(1)} all-gather(bf16[8,2048]{1,0:T(8,128)(2,1)} %param.14), channel_id=1, replica_groups=mesh['groups'=2,'role'=4,'tp'=4] {'tp'}, dimensions={0}, use_global_device_ids=true | all-gather | bytes 163840 | tf_op jit(solution)/shard_map/all_gather | solution.py:100
  22.1 5.7 %psum.28 = f32[32]{0:T(128)S(1)} all-reduce(f32[32]{0:T(128)S(1)} %fusion.11), channel_id=1, replica_groups=mesh['groups'=2,'role'=4,'tp'=4] {'role'}, use_global_device_ids=true, to_apply=%region_1.0 | all-reduce | flops 32 | bytes 256 | tf_op jit(solution)/shard_map/psum | solution.py:102
  27.8 1.3 convolution_convert_fusion.6
  29.1 1.3 convolution_convert_fusion.5
  30.4 3.1 %convolution_convert_fusion.4 = bf16[32,1024]{1,0:T(8,128)(2,1)S(1)} fusion(bf16[2048,1024]{1,0:T(8,128)(2,1)} %param.16, bf16[32,2048]{1,0:T(8,128)(2,1)S(1)} %all_gather.6, f32[2048]{0:T(1024)} %param.15, f32[32]{0:T(128)S(1)} %add_rsqrt_fusion.1), kind=kOutput, calls=%fused_computation.4 | convolution fusion | flops 134512640 | bytes 4399232 | tf_op jit(solution)/shard_map/dot_general | solution.py:107
  33.5 0.6 pad_maximum_fusion
  34.2 0.7 convert_element_type.97
  35.0 20.6 %reduce-scatter.4.cloned.1.call-done = bf16[8,1280]{1,0:T(8,128)(2,1)} async-done(((bf16[32,1280]{1,0:T(8,128)(2,1)}), bf16[8,1280]{1,0:T(8,128)(2,1)}) %reduce-scatter.4.cloned.1.call-update) | async-done | bytes 20496 | tf_op jit(solution)/shard_map/reduce_scatter | solution.py:113
  55.5 1.3 all_to_all.22
  56.9 4.6 %all-to-all-start = ((bf16[4,2,1280]{2,1,0:T(2,128)(2,1)}), bf16[4,2,1280]{2,1,0:T(2,128)(2,1)S(1)}, u32[]{:S(2)}, u32[]{:S(2)}) async-start(bf16[4,2,1280]{2,1,0:T(2,128)(2,1)} %all_to_all.22), calls=%async_computation.1 | async-start | bytes 40960 | tf_op jit(solution)/shard_map/all_to_all | solution.py:116
  61.5 0.7 iota_compare_fusion
  62.2 4.9 %all-to-all-done = bf16[4,2,1280]{2,1,0:T(2,128)(2,1)S(1)} async-done(((bf16[4,2,1280]{2,1,0:T(2,128)(2,1)}), bf16[4,2,1280]{2,1,0:T(2,128)(2,1)S(1)}, u32[]{:S(2)}, u32[]{:S(2)}) %all-to-all-start) | async-done | bytes 20512 | tf_op jit(solution)/shard_map/all_to_all | solution.py:116
  67.4 0.2 fusion.26
  67.6 0.3 fusion.39
  67.9 0.2 fusion.19
  68.2 1.3 fusion.1
  69.5 8.0 %all_to_all.29 = bf16[2,4,1024]{2,0,1:T(2,128)(2,1)S(1)} all-to-all(bf16[2,4,1024]{2,0,1:T(2,128)(2,1)S(1)} %copy.30), channel_id=1, replica_groups=mesh['groups'=2,'role'=4,'tp'=4] {'tp'}, dimensions={1} | all-to-all | bytes 32768 | tf_op jit(solution)/shard_map/all_to_all | solution.py:135
  77.5 5.2 %all_gather.7 = bf16[32,1024]{1,0:T(8,128)(2,1)S(1)} all-gather(bf16[8,1024]{1,0:T(8,128)(2,1)S(1)} %all_to_all.26), channel_id=1, replica_groups=mesh['groups'=2,'role'=4,'tp'=4] {'role'}, dimensions={0}, use_global_device_ids=true | all-gather | bytes 81920 | tf_op jit(solution)/shard_map/all_gather | solution.py:137
  82.7 3.7 %convolution_convert_fusion.3 = bf16[32,2048]{1,0:T(8,128)(2,1)} fusion(bf16[32,1024]{1,0:T(8,128)(2,1)S(1)} %all_gather.7, bf16[1024,2048]{1,0:T(8,128)(2,1)} %param.19), kind=kOutput, calls=%fused_computation.3 | convolution fusion | flops 134283264 | bytes 4390912 | tf_op jit(solution)/shard_map/dot_general | solution.py:136
  86.4 0.7 dynamic-slice_convert_fusion
  87.2 16.2 %reduce-scatter.6.cloned.1.call-done = bf16[8,2048]{1,0:T(8,128)(2,1)} async-done(((bf16[32,2048]{1,0:T(8,128)(2,1)}), bf16[8,2048]{1,0:T(8,128)(2,1)}) %reduce-scatter.6.cloned.1.call-update) | async-done | bytes 32784 | tf_op jit(solution)/shard_map/reduce_scatter | solution.py:141
  103.3 0.8 add_convert_fusion.1
  104.2 5.7 %collective-permute-done = bf16[8,2048]{1,0:T(8,128)(2,1)S(1)} collective-permute-done((bf16[8,2048]{1,0:T(8,128)(2,1)S(1)}, bf16[8,2048]{1,0:T(8,128)(2,1)S(1)}, u32[]{:S(2)}, u32[]{:S(2)}) %collective-permute-start) | collective-permute-done | bytes 32800 | tf_op jit(solution)/shard_map/ppermute | solution.py:147
  110.0 6.0 %collective-permute-done.1 = bf16[8,2048]{1,0:T(8,128)(2,1)S(1)} collective-permute-done((bf16[8,2048]{1,0:T(8,128)(2,1)S(1)}, bf16[8,2048]{1,0:T(8,128)(2,1)S(1)}, u32[]{:S(2)}, u32[]{:S(2)}) %collective-permute-start.1) | collective-permute-done | bytes 32800 | tf_op jit(solution)/shard_map/ppermute | solution.py:147
  115.9 5.7 %collective-permute-done.2 = bf16[8,2048]{1,0:T(8,128)(2,1)S(1)} collective-permute-done((bf16[8,2048]{1,0:T(8,128)(2,1)S(1)}, bf16[8,2048]{1,0:T(8,128)(2,1)S(1)}, u32[]{:S(2)}, u32[]{:S(2)}) %collective-permute-start.2) | collective-permute-done | bytes 32800 | tf_op jit(solution)/shard_map/ppermute | solution.py:147
  121.9 5.7 %psum.29 = f32[32]{0:T(128)S(1)} all-reduce(f32[32]{0:T(128)S(1)} %fusion.14), channel_id=1, replica_groups=mesh['groups'=2,'role'=4,'tp'=4] {'role'}, use_global_device_ids=true, to_apply=%region_7.8 | all-reduce | flops 32 | bytes 256 | tf_op jit(solution)/shard_map/psum | solution.py:64
  127.5 8.5 %convolution_convert_fusion = bf16[32,3584]{1,0:T(8,128)(2,1)} fusion(bf16[2048,3584]{1,0:T(8,128)(2,1)} %param.26, f32[2048]{0:T(1024)} %param.24, f32[32]{0:T(128)S(1)} %add_rsqrt_fusion, bf16[64,2048]{1,0:T(8,128)(2,1)S(1)} %constant_dynamic-update-slice_fusion, s32[]{:T(128)S(6)} %select_n.23), kind=kOutput, calls=%fused_computation | convolution fusion | flops 470138880 | bytes 15049220 | tf_op jit(solution)/shard_map/dot_general | solution.py:68
  136.1 8.5 %convolution_convert_fusion.1 = bf16[32,3584]{1,0:T(8,128)(2,1)} fusion(bf16[2048,3584]{1,0:T(8,128)(2,1)} %param.25, f32[2048]{0:T(1024)S(1)} %copy-done.1, f32[32]{0:T(128)S(1)} %add_rsqrt_fusion, bf16[64,2048]{1,0:T(8,128)(2,1)S(1)} %constant_dynamic-update-slice_fusion, s32[]{:T(128)S(6)} %select_n.23), kind=kOutput, calls=%fused_computation.1 | convolution fusion | flops 470138880 | bytes 15049220 | tf_op jit(solution)/shard_map/dot_general | solution.py:67
  144.7 31.7 %all-reduce.3.cloned.1.call-done = (bf16[32,3584]{1,0:T(8,128)(2,1)}, bf16[32,3584]{1,0:T(8,128)(2,1)}) async-done(((bf16[32,3584]{1,0:T(8,128)(2,1)}, bf16[32,3584]{1,0:T(8,128)(2,1)}), (bf16[32,3584]{1,0:T(8,128)(2,1)}, bf16[32,3584]{1,0:T(8,128)(2,1)})) %all-reduce.3.cloned.1.call-update) | async-done | bytes 458768 | tf_op jit(solution)/shard_map/psum | solution.py:71
  176.4 8.7 %convolution_convert_fusion.2 = bf16[32,2048]{1,0:T(8,128)(2,1)} fusion(bf16[3584,2048]{1,0:T(8,128)(2,1)} %param.27, bf16[32,3584]{1,0:T(8,128)(2,1)} %get-tuple-element.5, bf16[32,3584]{1,0:T(8,128)(2,1)} %get-tuple-element.6), kind=kOutput, calls=%fused_computation.2 | convolution fusion | flops 470745088 | bytes 15269888 | tf_op jit(solution)/shard_map/dot_general | solution.py:74
  185.1 19.6 %reduce-scatter.8.cloned.1.call-done = bf16[8,2048]{1,0:T(8,128)(2,1)} async-done(((bf16[32,2048]{1,0:T(8,128)(2,1)}), bf16[8,2048]{1,0:T(8,128)(2,1)}) %reduce-scatter.8.cloned.1.call-update) | async-done | bytes 32784 | tf_op jit(solution)/shard_map/reduce_scatter | solution.py:75
  204.7 1.4 add_convert_fusion
  (41 shorter events, 1.0 us)
Async XLA Ops:
  6.5 61.1 %copy-start = (bf16[2,256,512]{2,1,0:T(8,128)(2,1)S(1)}, bf16[2,256,512]{2,1,0:T(8,128)(2,1)}, u32[]{:S(2)}) copy-start(bf16[2,256,512]{2,1,0:T(8,128)(2,1)} %param.20) | copy-start | bytes 1572868
  6.5 49.0 %reduce-scatter.4.cloned.1.call-start = ((), (), s32[]{:S(2)}) async-start(), calls=%async_computation.5 | async-start | bytes 102400 | tf_op jit(solution)/shard_map/reduce_scatter | solution.py:113
  56.9 10.2 %all-to-all-start = ((bf16[4,2,1280]{2,1,0:T(2,128)(2,1)}), bf16[4,2,1280]{2,1,0:T(2,128)(2,1)S(1)}, u32[]{:S(2)}, u32[]{:S(2)}) async-start(bf16[4,2,1280]{2,1,0:T(2,128)(2,1)} %all_to_all.22), calls=%async_computation.1 | async-start | bytes 40960 | tf_op jit(solution)/shard_map/all_to_all | solution.py:116
  61.5 41.9 %reduce-scatter.6.cloned.1.call-start = ((), (), s32[]{:S(2)}) async-start(), calls=%async_computation.6 | async-start | bytes 163840 | tf_op jit(solution)/shard_map/reduce_scatter | solution.py:141
  67.6 68.5 %copy-start.1 = (f32[2048]{0:T(1024)S(1)}, f32[2048]{0:T(1024)}, u32[]{:S(2)}) copy-start(f32[2048]{0:T(1024)} %param.24) | copy-start | bytes 24580
  86.4 90.0 %all-reduce.3.cloned.1.call-start = ((), (), s32[]{:S(2)}) async-start(), calls=%async_computation.8 | async-start | bytes 917504 | tf_op jit(solution)/shard_map/psum | solution.py:71
  104.2 5.8 %collective-permute-start = (bf16[8,2048]{1,0:T(8,128)(2,1)S(1)}, bf16[8,2048]{1,0:T(8,128)(2,1)S(1)}, u32[]{:S(2)}, u32[]{:S(2)}) collective-permute-start(bf16[8,2048]{1,0:T(8,128)(2,1)S(1)} %add_convert_fusion.1), channel_id=1, source_target_pairs={{0,1},{1,2},{2,3},{3,0},{4,5},{5,6},{6,7},{7,4},{8,9},{9,10},{10,1... | collective-permute-start | bytes 98312 | tf_op jit(solution)/shard_map/ppermute | solution.py:147
  109.9 6.0 %collective-permute-start.1 = (bf16[8,2048]{1,0:T(8,128)(2,1)S(1)}, bf16[8,2048]{1,0:T(8,128)(2,1)S(1)}, u32[]{:S(2)}, u32[]{:S(2)}) collective-permute-start(bf16[8,2048]{1,0:T(8,128)(2,1)S(1)} %collective-permute-done), channel_id=1, source_target_pairs={{0,1},{1,2},{2,3},{3,0},{4,5},{5,6},{6,7},{7,4},{8,9},{9,10},{10,1... | collective-permute-start | bytes 98312 | tf_op jit(solution)/shard_map/ppermute | solution.py:147
  115.9 5.7 %collective-permute-start.2 = (bf16[8,2048]{1,0:T(8,128)(2,1)S(1)}, bf16[8,2048]{1,0:T(8,128)(2,1)S(1)}, u32[]{:S(2)}, u32[]{:S(2)}) collective-permute-start(bf16[8,2048]{1,0:T(8,128)(2,1)S(1)} %collective-permute-done.1), channel_id=1, source_target_pairs={{0,1},{1,2},{2,3},{3,0},{4,5},{5,6},{6,7},{7,4},{8,9},{9,10},{10,1... | collective-permute-start | bytes 98312 | tf_op jit(solution)/shard_map/ppermute | solution.py:147
  144.6 60.1 %reduce-scatter.8.cloned.1.call-start = ((), (), s32[]{:S(2)}) async-start(), calls=%async_computation.7 | async-start | bytes 163840 | tf_op jit(solution)/shard_map/reduce_scatter | solution.py:75
Sparse Core Ops, SparseCore 0:
  34.3 21.1 reduce-scatter.3
  86.5 16.7 reduce-scatter.5
  144.7 31.6 all-reduce.2
  185.3 19.4 reduce-scatter.7
